TPU v7x, 32 devices: a whole 2x2x4 slice. The times are simulated.
32 devices in a mesh: dp: 2 (over core), expert: 4 (over y, x), mp: 4 (over z).
Axes of the slice: x: 2, y: 2, z: 4, core: 2. Of those that a mesh axis runs over, the one named last changes fastest.
Arguments:
- tokens: bfloat16 [512, 3072], P(('dp', 'expert')), may hold values from -6 to 6
- w_router: float32 [3072, 4], replicated, may hold values from -0.109375 to 0.109375
- expert_ids: int32 [512, 2], P(('dp', 'expert')), may hold values from 0 to 3, all different within a row; in each aligned block of 64 rows (0 to 63, 64 to 127, ...) at most 64 rows name the same one
- partner: int32 [4], replicated, may hold values from 0 to 3, as said below
- gate_weight: bfloat16 [4, 3072, 8192], P('expert', None, ('dp', 'mp')), may hold values from -0.109375 to 0.109375
- up_weight: bfloat16 [4, 3072, 8192], P('expert', None, ('dp', 'mp')), may hold values from -0.109375 to 0.109375
- down_weight: bfloat16 [4, 8192, 3072], P('expert', ('dp', 'mp')), may hold values from -0.0625 to 0.0625
- grad_out: bfloat16 [512, 3072], P(('dp', 'expert')), may hold values from -1.5 to 1.5
Outputs:
- mixed: bfloat16 [512, 3072], P(('dp', 'expert'))
- grad_tokens: bfloat16 [512, 3072], P(('dp', 'expert'))
- grad_router: float32 [3072, 4], replicated
- grad_gate: bfloat16 [4, 3072, 8192], P('expert', None, ('dp', 'mp'))
- grad_up: bfloat16 [4, 3072, 8192], P('expert', None, ('dp', 'mp'))
- grad_down: bfloat16 [4, 8192, 3072], P('expert', ('dp', 'mp'))
Inputs may be any that keep to these rules, and one draw needn't show every extreme that they name: `expert_ids`: each token names two different experts. Within each aligned block of 64 tokens no expert is named by more than 64 tokens, and in every draw some block names some expert exactly 64 times. A matching of the experts: partner[partner[e]] = e and partner[e] != e for every expert e.
All inputs are finite; a program needn't handle non-finite values.
Results may differ from a plain program's by a relative error of at most 0.019.
Values may be sent and summed in bfloat16 or wider, within the bound.
No kernel may reach another device: no remote copies, remote signals or barrier semaphores. Data moves between devices by JAX's collectives and lax.ppermute only.
A program may use at most 128 MiB of HBM per device.

v0:
```python
import jax
import jax.numpy as jnp
from jax import lax
from jax.sharding import PartitionSpec as P

exact_mode = lax.Precision.HIGHEST


def local(tokens, w_router, expert_ids, partner, gate_weight, up_weight, down_weight, grad_out):
    tok_rows, features = tokens.shape
    experts = w_router.shape[1]
    hid_part = gate_weight.shape[2]
    dp_count = lax.axis_size("dp")
    exp_count = lax.axis_size("expert")
    slot_count = min(tok_rows, 4 * tok_rows // experts)
    keep_count = 3 * slot_count // 4
    slot_total = experts * slot_count
    block_rows = exp_count * slot_count
    floats = tokens.astype(jnp.float32)
    logits = jnp.dot(floats, w_router, precision=exact_mode)
    chosen = (expert_ids[:, :, None] == lax.iota(jnp.int32, experts)[None, None, :]).astype(
        jnp.int32
    )
    chosen_float = chosen.astype(jnp.float32)
    picked = jnp.sum(logits[:, None, :] * chosen_float, axis=2)
    share_one = jax.nn.sigmoid(picked[:, 0] - picked[:, 1])
    shares = jnp.stack([share_one, 1.0 - share_one], axis=1)
    flat_choice = chosen.reshape(2 * tok_rows, experts)
    earlier = jnp.cumsum(flat_choice, axis=0) - flat_choice
    arrival = jnp.sum(earlier * flat_choice, axis=1).reshape(tok_rows, 2)
    partner_of = jnp.sum(chosen * partner[None, None, :], axis=2)
    target = jnp.where(arrival < keep_count, expert_ids, partner_of)
    slot_index = target * slot_count + arrival
    placing = (slot_index[:, :, None] == lax.iota(jnp.int32, slot_total)[None, None, :]).astype(
        jnp.bfloat16
    )
    send_tokens = jnp.einsum("tks,td->sd", placing, tokens, preferred_element_type=jnp.float32)
    send_tokens = send_tokens.astype(jnp.bfloat16).reshape(experts, slot_count, features)
    scaled = (shares[:, :, None] * grad_out.astype(jnp.float32)[:, None, :]).astype(jnp.bfloat16)
    send_cot = jnp.einsum("tks,tkd->sd", placing, scaled, preferred_element_type=jnp.float32)
    send_cot = send_cot.astype(jnp.bfloat16).reshape(experts, slot_count, features)

    def spread(buffer):
        arrived = lax.all_to_all(buffer, "expert", split_axis=0, concat_axis=0, tiled=True)
        return lax.all_gather(arrived, "dp", axis=0, tiled=True)

    rows_in = spread(send_tokens).reshape(-1, features)
    pieces = 1

    def combine(partial_value):
        summed = lax.psum(
            partial_value.reshape(dp_count, block_rows, features).astype(jnp.bfloat16), ("dp", "mp")
        ).astype(jnp.float32)
        own_rows = lax.dynamic_index_in_dim(summed, lax.axis_index("dp"), 0, keepdims=False)
        own_rows = own_rows.astype(jnp.bfloat16).reshape(exp_count, slot_count, features)
        restored = lax.all_to_all(own_rows, "expert", split_axis=0, concat_axis=0, tiled=True)
        return restored.reshape(slot_total, features)

    w_gate = gate_weight[0]
    w_up = up_weight[0]
    w_down = down_weight[0]
    pre_gate = jnp.dot(rows_in, w_gate, preferred_element_type=jnp.float32)
    pre_up = jnp.dot(rows_in, w_up, preferred_element_type=jnp.float32)
    sigmoid_gate = jax.nn.sigmoid(pre_gate)
    swished = pre_gate * sigmoid_gate
    hidden = (swished * pre_up).astype(jnp.bfloat16)
    down_split = w_down.reshape(hid_part, pieces, features // pieces)
    forward_terms = jnp.einsum(
        "prf,fqd->pqrd",
        hidden.reshape(dp_count, block_rows, hid_part),
        down_split,
        preferred_element_type=jnp.float32,
    )
    expert_out = combine(forward_terms)
    back_rows = jnp.einsum("tks,sd->tkd", placing, expert_out, preferred_element_type=jnp.float32)
    mixed = (shares[:, 0, None] * back_rows[:, 0] + shares[:, 1, None] * back_rows[:, 1]).astype(
        jnp.bfloat16
    )
    falling = grad_out.astype(jnp.float32)
    dshare = jnp.sum(falling[:, None, :] * back_rows, axis=2)
    dlogit = shares[:, 0] * shares[:, 1] * (dshare[:, 0] - dshare[:, 1])
    grad_logits = (chosen_float[:, 0] - chosen_float[:, 1]) * dlogit[:, None]
    router_term = lax.dot_general(
        floats, grad_logits, (((0,), (0,)), ((), ())), precision=exact_mode
    )
    grad_router = lax.psum(router_term.astype(jnp.bfloat16), ("dp", "expert")).astype(jnp.float32)
    router_back = jnp.dot(grad_logits, w_router.T, precision=exact_mode)
    cot_in = spread(send_cot).reshape(-1, features)
    dhidden = jnp.einsum("rd,fd->rf", cot_in, w_down, preferred_element_type=jnp.float32)
    up_grad = (dhidden * swished).astype(jnp.bfloat16)
    gate_grad = (dhidden * pre_up * sigmoid_gate * (1.0 + pre_gate * (1.0 - sigmoid_gate))).astype(
        jnp.bfloat16
    )
    grad_down = jnp.einsum("rf,rd->fd", hidden, cot_in, preferred_element_type=jnp.float32).astype(
        jnp.bfloat16
    )[None]
    grad_gate = jnp.einsum(
        "rd,rf->df", rows_in, gate_grad, preferred_element_type=jnp.float32
    ).astype(jnp.bfloat16)[None]
    grad_up = jnp.einsum("rd,rf->df", rows_in, up_grad, preferred_element_type=jnp.float32).astype(
        jnp.bfloat16
    )[None]
    gate_split = w_gate.reshape(pieces, features // pieces, hid_part)
    up_split = w_up.reshape(pieces, features // pieces, hid_part)
    backward_terms = jnp.einsum(
        "prf,qdf->pqrd",
        gate_grad.reshape(dp_count, block_rows, hid_part),
        gate_split,
        preferred_element_type=jnp.float32,
    )
    backward_terms = backward_terms + jnp.einsum(
        "prf,qdf->pqrd",
        up_grad.reshape(dp_count, block_rows, hid_part),
        up_split,
        preferred_element_type=jnp.float32,
    )
    row_grads = combine(backward_terms)
    grad_rows = jnp.einsum("tks,sd->tkd", placing, row_grads, preferred_element_type=jnp.float32)
    grad_tokens = (router_back + grad_rows[:, 0] + grad_rows[:, 1]).astype(jnp.bfloat16)
    return (mixed, grad_tokens, grad_router, grad_gate, grad_up, grad_down)


def solution(mesh):
    in_specs = (
        P(("dp", "expert"), None),
        P(),
        P(("dp", "expert"), None),
        P(),
        P("expert", None, ("dp", "mp")),
        P("expert", None, ("dp", "mp")),
        P("expert", ("dp", "mp"), None),
        P(("dp", "expert"), None),
    )
    out_specs = (
        P(("dp", "expert"), None),
        P(("dp", "expert"), None),
        P(),
        P("expert", None, ("dp", "mp")),
        P("expert", None, ("dp", "mp")),
        P("expert", ("dp", "mp"), None),
    )
    return jax.shard_map(local, mesh=mesh, in_specs=in_specs, out_specs=out_specs, check_vma=False)
```

profile of v0, /device:TPU:1, one launch (start us, length us, event | category | flops | bytes accessed | tf_op | source)
XLA Modules:
  0.0 329.8 jit_solution(508223752091180420)
XLA Ops:
  7.2 0.0 copy-start
  7.2 0.0 all-gather.5.cloned.1.call-start
  7.2 0.8 copy.29
  8.0 0.1 copy-done
  8.2 1.2 fusion.42
  9.4 0.7 multiply_reduce_fusion.1
  10.1 0.1 eq.38
  10.3 0.1 fusion.34
  10.4 0.2 reduce_window_sum.11
  10.5 0.2 select_reduce_fusion
  10.7 0.1 reshape.71
  10.9 0.1 copy.30
  10.9 0.8 select_reduce_fusion.1
  11.7 1.0 convert_element_type.104
  12.8 0.7 fusion.38
  13.5 0.7 fusion.17
  14.2 22.7 %all_to_all.20 = bf16[4,64,3072]{2,1,0:T(8,128)(2,1)} all-to-all(bf16[4,64,3072]{2,1,0:T(8,128)(2,1)S(1)} %bitcast.108), channel_id=1, replica_groups=mesh['dp'=2,'expert'=4,'mp'=4] {'expert'}, dimensions={0} | all-to-all | bytes 3145728 | tf_op jit(solution)/shard_map/all_to_all | solution.py:44
  36.8 0.0 all-gather.5.cloned.1.call-update
  36.9 0.0 all-gather.3.cloned.1.call-start
  36.9 0.1 convert_reduce_fusion
  37.0 0.6 fusion.43
  37.6 20.3 %all_to_all.21 = bf16[4,64,3072]{2,1,0:T(8,128)(2,1)} all-to-all(bf16[4,64,3072]{2,1,0:T(8,128)(2,1)S(1)} %bitcast.105), channel_id=1, replica_groups=mesh['dp'=2,'expert'=4,'mp'=4] {'expert'}, dimensions={0} | all-to-all | bytes 3145728 | tf_op jit(solution)/shard_map/all_to_all | solution.py:44
  57.9 0.0 all-gather.3.cloned.1.call-update
  57.9 0.0 all-reduce.3.cloned.1.call-start
  58.0 0.0 all-gather.5.cloned.1.call-done
  58.0 6.5 %fusion.6 = f32[512,1024]{1,0:T(8,128)S(1)} fusion(bf16[512,3072]{1,0:T(8,128)(2,1)} %bitcast.120, bf16[1,1024,3072]{2,1,0:T(8,128)(2,1)} %param.14), kind=kOutput, calls=%fused_computation.6 | convolution fusion | flops 3221225472 | bytes 11534336 | tf_op jit(solution)/shard_map/rd,fd->rf/dot_general | solution.py:89
  64.6 8.7 %all-gather.3.cloned.1.call-done = bf16[8,64,3072]{2,1,0:T(8,128)(2,1)} async-done(((bf16[4,64,3072]{2,1,0:T(8,128)(2,1)}), bf16[8,64,3072]{2,1,0:T(8,128)(2,1)}) %all-gather.3.cloned.1.call-update) | async-done | bytes 3145744 | tf_op jit(solution)/shard_map/all_gather | solution.py:45
  73.3 6.6 %fusion.8 = f32[512,1024]{1,0:T(8,128)S(1)} fusion(bf16[512,3072]{1,0:T(8,128)(2,1)} %bitcast.116, bf16[1,3072,1024]{2,1,0:T(8,128)(2,1)} %param.13), kind=kOutput, calls=%fused_computation.8 | convolution fusion | flops 3221225472 | bytes 11534336 | tf_op jit(solution)/shard_map/dot_general | solution.py:63
  79.9 0.0 copy-done.5
  79.9 0.0 slice-start.1
  79.9 0.0 slice-start.3
  79.9 0.0 slice-start.4
  79.9 7.3 %multiply_convert_fusion.1 = (bf16[512,1024]{1,0:T(8,128)(2,1)S(1)}, bf16[512,1024]{1,0:T(8,128)(2,1)S(1)}, bf16[512,1024]{1,0:T(8,128)(2,1)S(1)}) fusion(f32[512,1024]{1,0:T(8,128)S(1)} %fusion.6, f32[512,1024]{1,0:T(8,128)S(1)} %fusion.8, bf16[512,3072]{1,0:T(8,128)(2,1)S(1)} %bitcast.118, bf16[1,3072,1024]{2,1,0:T(8,128)(2,1)} %param.12), kind=kOutput, calls=%fused_computation.28 | convolution fusion | flops 3229089792 | bytes 16777216 | tf_op jit(solution)/shard_map/dot_general | solution.py:62
  87.2 0.0 copy-start.9
  87.2 0.0 copy-start.10
  87.2 0.0 copy-start.7
  87.3 0.0 slice-done
  87.3 0.0 slice-done.1
  87.3 0.0 slice-start.5
  87.3 5.4 %fusion = f32[2,256,3072]{2,1,0:T(8,128)} fusion(bf16[2,256,1024]{2,1,0:T(8,128)(2,1)S(1)} %bitcast.123, bf16[1,3072,1024]{2,1,0:T(8,128)(2,1)S(1)} %bitcast.111), kind=kOutput, calls=%fused_computation | convolution fusion | flops 3221225472 | bytes 13631488 | tf_op jit(solution)/shard_map/prf,qdf->pqrd/dot_general | solution.py:111
  92.7 0.0 copy-done.9
  92.7 0.0 slice-done.3
  92.7 4.8 %fusion.14 = bf16[2,256,3072]{2,1,0:T(8,128)(2,1)} fusion(bf16[2,256,1024]{2,1,0:T(8,128)(2,1)S(1)} %bitcast.124, bf16[1,1024,3072]{2,1,0:T(8,128)(2,1)S(1)} %bitcast.113), kind=kOutput, calls=%fused_computation.16 | convolution fusion | flops 3222798336 | bytes 10485760 | tf_op jit(solution)/shard_map/prf,fqd->pqrd/dot_general | solution.py:68
  97.5 0.0 slice-done.4
  97.5 6.8 %add_convert_fusion = bf16[2,256,3072]{2,1,0:T(8,128)(2,1)} fusion(f32[2,256,3072]{2,1,0:T(8,128)} %fusion, bf16[2,256,1024]{2,1,0:T(8,128)(2,1)S(1)} %bitcast.122, bf16[1,3072,1024]{2,1,0:T(8,128)(2,1)S(1)} %bitcast.115), kind=kOutput, calls=%fused_computation.15 | convolution fusion | flops 3224371200 | bytes 16777216 | tf_op jit(solution)/shard_map/prf,qdf->pqrd/dot_general | solution.py:105
  104.3 0.0 all-reduce.3.cloned.1.call-update
  104.4 137.3 %all-reduce.3.cloned.1.call-done = (bf16[2,256,3072]{2,1,0:T(8,128)(2,1)}, bf16[2,256,3072]{2,1,0:T(8,128)(2,1)}) async-done(((bf16[2,256,3072]{2,1,0:T(8,128)(2,1)}, bf16[2,256,3072]{2,1,0:T(8,128)(2,1)}), (bf16[2,256,3072]{2,1,0:T(8,128)(2,1)}, bf16[2,256,3072]{2,1,0:T(8,128)(2,1)})) %all-reduce.3.cloned.1.call-update) | async-done | bytes 6291472 | tf_op jit(solution)/shard_map/psum | solution.py:51
  241.6 2.7 convert_convert_fusion
  244.3 3.7 %all-to-all-start.3 = ((bf16[4,64,3072]{2,1,0:T(8,128)(2,1)}), bf16[4,64,3072]{2,1,0:T(8,128)(2,1)S(1)}, u32[]{:S(2)}, u32[]{:S(2)}) async-start(bf16[4,64,3072]{2,1,0:T(8,128)(2,1)} %bitcast.107), calls=%async_computation.3 | async-start | bytes 3145728 | tf_op jit(solution)/shard_map/all_to_all | solution.py:56
  248.1 0.0 copy-done.4
  248.1 8.5 %convert_bitcast_fusion = bf16[1,1024,3072]{2,1,0:T(8,128)(2,1)} fusion(bf16[512,1024]{1,0:T(8,128)(2,1)} %copy-done.10, bf16[512,3072]{1,0:T(8,128)(2,1)} %bitcast.121), kind=kOutput, calls=%fused_computation.12 | convolution fusion | flops 3224371200 | bytes 10485760 | tf_op jit(solution)/shard_map/rf,rd->fd/dot_general | solution.py:94
  256.6 1.3 convert_convert_fusion.1
  257.9 8.6 %all-to-all-done.3 = bf16[4,64,3072]{2,1,0:T(8,128)(2,1)S(1)} async-done(((bf16[4,64,3072]{2,1,0:T(8,128)(2,1)}), bf16[4,64,3072]{2,1,0:T(8,128)(2,1)S(1)}, u32[]{:S(2)}, u32[]{:S(2)}) %all-to-all-start.3) | async-done | bytes 1572896 | tf_op jit(solution)/shard_map/all_to_all | solution.py:56
  266.6 4.4 %all-to-all-start.1 = ((bf16[4,64,3072]{2,1,0:T(8,128)(2,1)}), bf16[4,64,3072]{2,1,0:T(8,128)(2,1)}, u32[]{:S(2)}, u32[]{:S(2)}) async-start(bf16[4,64,3072]{2,1,0:T(8,128)(2,1)} %bitcast.106), calls=%async_computation.1 | async-start | bytes 3145728 | tf_op jit(solution)/shard_map/all_to_all | solution.py:56
  270.9 8.5 %convert_bitcast_fusion.1 = bf16[1,3072,1024]{2,1,0:T(8,128)(2,1)} fusion(bf16[512,3072]{1,0:T(8,128)(2,1)} %bitcast.117, bf16[512,1024]{1,0:T(8,128)(2,1)} %copy-done.9), kind=kOutput, calls=%fused_computation.13 | convolution fusion | flops 3224371200 | bytes 10485760 | tf_op jit(solution)/shard_map/rd,rf->df/dot_general | solution.py:100
  279.5 5.4 %convert_bitcast_fusion.2 = bf16[1,3072,1024]{2,1,0:T(8,128)(2,1)} fusion(bf16[512,3072]{1,0:T(8,128)(2,1)S(1)} %bitcast.119, bf16[512,1024]{1,0:T(8,128)(2,1)S(1)} %copy-done.8), kind=kOutput, calls=%fused_computation.14 | convolution fusion | flops 3224371200 | bytes 10485760 | tf_op jit(solution)/shard_map/rd,rf->df/dot_general | solution.py:97
  284.8 1.6 fusion.28
  286.4 3.3 all-to-all-done.1
  289.7 2.1 multiply_reduce_fusion
  291.8 0.3 fusion.20
  292.0 1.6 fusion.19
  293.7 28.0 %psum.23 = bf16[3072,4]{0,1:T(4,128)(2,1)S(1)} all-reduce(bf16[3072,4]{0,1:T(4,128)(2,1)S(1)} %fusion.20), channel_id=1, replica_groups=mesh['dp'=2,'expert'=4,'mp'=4] {'dp','expert'}, use_global_device_ids=true, to_apply=%region_8.9 | all-reduce | flops 12288 | bytes 49152 | tf_op jit(solution)/shard_map/psum | solution.py:86
  321.7 0.6 convert_element_type.116
  322.3 0.9 fusion.24
  (26 shorter events, 0.1 us)
Async XLA Ops:
  7.2 1.0 copy-start
  7.2 50.8 %all-gather.5.cloned.1.call-start = ((), (), s32[]{:S(2)}) async-start(), calls=%async_computation.5 | async-start | bytes 4718592 | tf_op jit(solution)/shard_map/all_gather | solution.py:45
  36.9 36.4 %all-gather.3.cloned.1.call-start = ((), (), s32[]{:S(2)}) async-start(), calls=%async_computation.4 | async-start | bytes 4718592 | tf_op jit(solution)/shard_map/all_gather | solution.py:45
  57.9 183.7 %all-reduce.3.cloned.1.call-start = ((), (), s32[]{:S(2)}) async-start(), calls=%async_computation.6 | async-start | bytes 12582912 | tf_op jit(solution)/shard_map/psum | solution.py:51
  73.3 6.6 %copy-start.5 = (bf16[8,64,3072]{2,1,0:T(8,128)(2,1)S(1)}, bf16[8,64,3072]{2,1,0:T(8,128)(2,1)}, u32[]{:S(2)}) copy-start(bf16[8,64,3072]{2,1,0:T(8,128)(2,1)} %all-gather.3.cloned.1.call-done) | copy-start | bytes 9437188
  73.3 14.0 %slice-start = ((s8[6291456]{0:T(1024)(128)(4,1)}), s8[4194304]{0:T(1024)(128)(4,1)S(1)}, s32[]{:S(2)}) async-start(s8[6291456]{0:T(1024)(128)(4,1)} %bitcast.110), calls=%async_computation.7 | async-start | bytes 8388608
  73.3 19.4 %slice-start.2 = ((s8[6291456]{0:T(1024)(128)(4,1)}), s8[4194304]{0:T(1024)(128)(4,1)S(1)}, s32[]{:S(2)}) async-start(s8[6291456]{0:T(1024)(128)(4,1)} %bitcast.112), calls=%async_computation.9 | async-start | bytes 8388608
  79.9 7.4 %slice-start.1 = ((s8[6291456]{0:T(1024)(128)(4,1)}), s8[2097152]{0:T(1024)(128)(4,1)S(1)}, s32[]{:S(2)}) async-start(s8[6291456]{0:T(1024)(128)(4,1)} %bitcast.110), calls=%async_computation.8 | async-start | bytes 4194304
  79.9 12.8 %slice-start.3 = ((s8[6291456]{0:T(1024)(128)(4,1)}), s8[2097152]{0:T(1024)(128)(4,1)S(1)}, s32[]{:S(2)}) async-start(s8[6291456]{0:T(1024)(128)(4,1)} %bitcast.112), calls=%async_computation.10 | async-start | bytes 4194304
  79.9 17.6 %slice-start.4 = ((s8[6291456]{0:T(1024)(128)(4,1)}), s8[4194304]{0:T(1024)(128)(4,1)S(1)}, s32[]{:S(2)}) async-start(s8[6291456]{0:T(1024)(128)(4,1)} %bitcast.114), calls=%async_computation.11 | async-start | bytes 8388608
  87.2 5.4 %copy-start.9 = (bf16[512,1024]{1,0:T(8,128)(2,1)}, bf16[512,1024]{1,0:T(8,128)(2,1)S(1)}, u32[]{:S(2)}) copy-start(bf16[512,1024]{1,0:T(8,128)(2,1)S(1)} %get-tuple-element.11) | copy-start | bytes 3145732
  87.2 5.4 %copy-start.10 = (bf16[512,1024]{1,0:T(8,128)(2,1)}, bf16[512,1024]{1,0:T(8,128)(2,1)S(1)}, u32[]{:S(2)}) copy-start(bf16[512,1024]{1,0:T(8,128)(2,1)S(1)} %get-tuple-element.12) | copy-start | bytes 3145732
  87.2 10.3 %copy-start.7 = (bf16[512,1024]{1,0:T(8,128)(2,1)}, bf16[512,1024]{1,0:T(8,128)(2,1)S(1)}, u32[]{:S(2)}) copy-start(bf16[512,1024]{1,0:T(8,128)(2,1)S(1)} %get-tuple-element.10) | copy-start | bytes 3145732
  87.3 10.2 %slice-start.5 = ((s8[6291456]{0:T(1024)(128)(4,1)}), s8[2097152]{0:T(1024)(128)(4,1)S(1)}, s32[]{:S(2)}) async-start(s8[6291456]{0:T(1024)(128)(4,1)} %bitcast.114), calls=%async_computation.12 | async-start | bytes 4194304
  241.6 6.4 %copy-start.4 = (s32[64,2]{0,1:T(2,128)S(1)}, s32[64,2]{0,1:T(2,128)}, u32[]{:S(2)}) copy-start(s32[64,2]{0,1:T(2,128)} %param.10) | copy-start | bytes 1540
  244.3 22.3 %all-to-all-start.3 = ((bf16[4,64,3072]{2,1,0:T(8,128)(2,1)}), bf16[4,64,3072]{2,1,0:T(8,128)(2,1)S(1)}, u32[]{:S(2)}, u32[]{:S(2)}) async-start(bf16[4,64,3072]{2,1,0:T(8,128)(2,1)} %bitcast.107), calls=%async_computation.3 | async-start | bytes 3145728 | tf_op jit(solution)/shard_map/all_to_all | solution.py:56
  248.1 8.6 %copy-start.2 = (bf16[2,256,3072]{2,1,0:T(8,128)(2,1)S(1)}, bf16[2,256,3072]{2,1,0:T(8,128)(2,1)}, u32[]{:S(2)}) copy-start(bf16[2,256,3072]{2,1,0:T(8,128)(2,1)} %get-tuple-element.6) | copy-start | bytes 9437188
  266.6 23.1 %all-to-all-start.1 = ((bf16[4,64,3072]{2,1,0:T(8,128)(2,1)}), bf16[4,64,3072]{2,1,0:T(8,128)(2,1)}, u32[]{:S(2)}, u32[]{:S(2)}) async-start(bf16[4,64,3072]{2,1,0:T(8,128)(2,1)} %bitcast.106), calls=%async_computation.1 | async-start | bytes 3145728 | tf_op jit(solution)/shard_map/all_to_all | solution.py:56
  270.9 8.5 %copy-start.6 = (bf16[8,64,3072]{2,1,0:T(8,128)(2,1)S(1)}, bf16[8,64,3072]{2,1,0:T(8,128)(2,1)}, u32[]{:S(2)}) copy-start(bf16[8,64,3072]{2,1,0:T(8,128)(2,1)} %all-gather.3.cloned.1.call-done) | copy-start | bytes 9437188
  270.9 8.5 %copy-start.8 = (bf16[512,1024]{1,0:T(8,128)(2,1)S(1)}, bf16[512,1024]{1,0:T(8,128)(2,1)}, u32[]{:S(2)}) copy-start(bf16[512,1024]{1,0:T(8,128)(2,1)} %copy-done.7) | copy-start | bytes 3145732
  284.8 7.2 %copy-start.3 = (f32[3072,4]{0,1:T(4,128)S(1)}, f32[3072,4]{0,1:T(4,128)}, u32[]{:S(2)}) copy-start(f32[3072,4]{0,1:T(4,128)} %param.9) | copy-start | bytes 147460
  289.7 2.4 copy-start.1
Sparse Core Ops, SparseCore 0:
  37.0 13.7 all-gather.4
  58.1 15.1 all-gather.2
  104.5 137.1 all-reduce.2
where the time goes:
time: 330 us
  waiting for transfers between devices  158 us (48%)
  blocking collectives  71 us (22%)
  matrix products  67.8 us (21%)
  between operations  14.1 us (4%)
  other arithmetic  9.3 us (3%)
  starting transfers between devices  8.22 us (2%)
    psum x1, waiting for transfers between devices, combine(): lax.psum(partial_value.reshape(dp_count, block_rows, features).astype(jnp...  137 us
    all_to_all x2, blocking collectives, spread(): lax.all_to_all(buffer, 'expert', split_axis=0, concat_axis=0, tiled=True)  43 us
    psum x1, blocking collectives, local(): lax.psum(router_term.astype(jnp.bfloat16), ('dp', 'expert'))  28 us
    all_to_all x2, waiting for transfers between devices, combine(): lax.all_to_all(own_rows, 'expert', split_axis=0, concat_axis=0, tiled=True)  11.9 us
    all_gather x2, waiting for transfers between devices, spread(): return lax.all_gather(arrived, 'dp', axis=0, tiled=True)  8.71 us
    dot_general x1, matrix products, local(): jnp.einsum('rf,rd->fd', hidden, cot_in, preferred_element_type=jnp.float32)  8.54 us
    dot_general x1, matrix products, local(): jnp.einsum('rd,rf->df', rows_in, up_grad, preferred_element_type=jnp.floa...  8.5 us
    all_to_all x2, starting transfers between devices, combine(): lax.all_to_all(own_rows, 'expert', split_axis=0, concat_axis=0, tiled=True)  8.1 us
  transfers between devices with their start and end apart: 5, of which 4 were waited for; matrix products, arithmetic and copies ran while one was open for 10% of the time, Pallas kernels for 0%

commit v1 on v0

--- a/solution.py
+++ b/solution.py
@@ -4,6 +4,11 @@
 from jax.sharding import PartitionSpec as P
 
 exact_mode = lax.Precision.HIGHEST
+
+
+def by_each_axis(array, axis_one, axis_two):
+    inner = lax.psum(array, axis_one)
+    return lax.psum(inner, axis_two)
 
 
 def local(tokens, w_router, expert_ids, partner, gate_weight, up_weight, down_weight, grad_out):
@@ -48,8 +53,8 @@
     pieces = 1
 
     def combine(partial_value):
-        summed = lax.psum(
-            partial_value.reshape(dp_count, block_rows, features).astype(jnp.bfloat16), ("dp", "mp")
+        summed = by_each_axis(
+            partial_value.reshape(dp_count, block_rows, features).astype(jnp.bfloat16), "mp", "dp"
         ).astype(jnp.float32)
         own_rows = lax.dynamic_index_in_dim(summed, lax.axis_index("dp"), 0, keepdims=False)
         own_rows = own_rows.astype(jnp.bfloat16).reshape(exp_count, slot_count, features)

time: 330 us -> 445 us (1.35)
  waiting for transfers between devices: 158 us -> 277 us
    psum x1 -> x2, waiting for transfers between devices: 137 us -> 258 us  [the longest x1 224 us: by_each_axis(): inner = lax.psum(array, axis_one)]
  transfers between devices with their start and end apart: 5 -> 6, of which waited for: 4 -> 5; matrix products, arithmetic and copies ran while one was open for 10% -> 8% of each run, Pallas kernels for 0% -> 0%
where the time goes in v1:
time: 445 us
  waiting for transfers between devices  277 us (62%)
  blocking collectives  71 us (16%)
  matrix products  63.4 us (14%)
  between operations  14.1 us (3%)
  other arithmetic  9.31 us (2%)
  starting transfers between devices  8.32 us (2%)
    psum x1, waiting for transfers between devices, by_each_axis(): inner = lax.psum(array, axis_one)  224 us
    all_to_all x2, blocking collectives, spread(): lax.all_to_all(buffer, 'expert', split_axis=0, concat_axis=0, tiled=True)  43 us
    psum x1, waiting for transfers between devices, by_each_axis(): return lax.psum(inner, axis_two)  33.8 us
    psum x1, blocking collectives, local(): lax.psum(router_term.astype(jnp.bfloat16), ('dp', 'expert'))  28 us
    all_to_all x2, waiting for transfers between devices, combine(): lax.all_to_all(own_rows, 'expert', split_axis=0, concat_axis=0, tiled=True)  12.4 us
  transfers between devices with their start and end apart: 6, of which 5 were waited for; matrix products, arithmetic and copies ran while one was open for 8% of the time, Pallas kernels for 0%

profile of v1, /device:TPU:1, one launch (start us, length us, event | category | flops | bytes accessed | tf_op | source)
XLA Modules:
  0.0 444.5 jit_solution(12461712634632548116)
XLA Ops:
  7.2 0.0 copy-start
  7.2 0.0 all-gather.5.cloned.1.call-start
  7.2 0.8 copy.29
  8.0 0.1 copy-done
  8.2 1.2 fusion.42
  9.4 0.7 multiply_reduce_fusion.1
  10.1 0.1 eq.38
  10.3 0.1 fusion.34
  10.4 0.2 reduce_window_sum.11
  10.5 0.2 select_reduce_fusion
  10.7 0.1 reshape.71
  10.9 0.1 copy.30
  10.9 0.8 select_reduce_fusion.1
  11.7 1.0 convert_element_type.104
  12.8 0.7 fusion.38
  13.5 0.7 fusion.17
  14.2 22.7 %all_to_all.20 = bf16[4,64,3072]{2,1,0:T(8,128)(2,1)} all-to-all(bf16[4,64,3072]{2,1,0:T(8,128)(2,1)S(1)} %bitcast.108), channel_id=1, replica_groups=mesh['dp'=2,'expert'=4,'mp'=4] {'expert'}, dimensions={0} | all-to-all | bytes 3145728 | tf_op jit(solution)/shard_map/all_to_all | solution.py:49
  36.8 0.0 all-gather.5.cloned.1.call-update
  36.9 0.0 all-gather.3.cloned.1.call-start
  36.9 0.1 convert_reduce_fusion
  37.0 0.6 fusion.43
  37.6 20.3 %all_to_all.21 = bf16[4,64,3072]{2,1,0:T(8,128)(2,1)} all-to-all(bf16[4,64,3072]{2,1,0:T(8,128)(2,1)S(1)} %bitcast.105), channel_id=1, replica_groups=mesh['dp'=2,'expert'=4,'mp'=4] {'expert'}, dimensions={0} | all-to-all | bytes 3145728 | tf_op jit(solution)/shard_map/all_to_all | solution.py:49
  57.9 0.0 all-gather.3.cloned.1.call-update
  57.9 0.0 all-reduce.5.cloned.1.call-start
  58.0 0.0 all-gather.5.cloned.1.call-done
  58.0 0.0 slice-start.4
  58.0 8.6 %fusion.6 = f32[512,1024]{1,0:T(8,128)} fusion(bf16[512,3072]{1,0:T(8,128)(2,1)} %bitcast.120, bf16[1,1024,3072]{2,1,0:T(8,128)(2,1)} %param.14), kind=kOutput, calls=%fused_computation.6 | convolution fusion | flops 3221225472 | bytes 11534336 | tf_op jit(solution)/shard_map/rd,fd->rf/dot_general | solution.py:94
  66.7 6.6 %all-gather.3.cloned.1.call-done = bf16[8,64,3072]{2,1,0:T(8,128)(2,1)} async-done(((bf16[4,64,3072]{2,1,0:T(8,128)(2,1)}), bf16[8,64,3072]{2,1,0:T(8,128)(2,1)}) %all-gather.3.cloned.1.call-update) | async-done | bytes 3145744 | tf_op jit(solution)/shard_map/all_gather | solution.py:50
  73.3 6.8 %fusion.8 = f32[512,1024]{1,0:T(8,128)S(1)} fusion(bf16[512,3072]{1,0:T(8,128)(2,1)} %bitcast.116, bf16[1,3072,1024]{2,1,0:T(8,128)(2,1)} %param.13), kind=kOutput, calls=%fused_computation.8 | convolution fusion | flops 3221225472 | bytes 11534336 | tf_op jit(solution)/shard_map/dot_general | solution.py:68
  80.1 0.0 slice-done.4
  80.1 0.0 slice-done.5
  80.1 0.0 copy-done.5
  80.1 0.0 slice-start.1
  80.1 0.0 slice-start.3
  80.1 4.4 multiply_convert_fusion.1
  84.5 0.0 copy-start.9
  84.5 0.0 copy-start.10
  84.5 0.0 copy-start.7
  84.6 3.5 fusion
  88.1 4.8 %fusion.14 = bf16[2,256,3072]{2,1,0:T(8,128)(2,1)} fusion(bf16[2,256,1024]{2,1,0:T(8,128)(2,1)S(1)} %bitcast.124, bf16[1,1024,3072]{2,1,0:T(8,128)(2,1)S(1)} %bitcast.113), kind=kOutput, calls=%fused_computation.16 | convolution fusion | flops 3222798336 | bytes 10485760 | tf_op jit(solution)/shard_map/prf,fqd->pqrd/dot_general | solution.py:73
  92.9 5.0 %add_convert_fusion = bf16[2,256,3072]{2,1,0:T(8,128)(2,1)} fusion(f32[2,256,3072]{2,1,0:T(8,128)S(1)} %fusion, bf16[2,256,1024]{2,1,0:T(8,128)(2,1)S(1)} %bitcast.122, bf16[1,3072,1024]{2,1,0:T(8,128)(2,1)S(1)} %bitcast.115), kind=kOutput, calls=%fused_computation.15 | convolution fusion | flops 3224371200 | bytes 16777216 | tf_op jit(solution)/shard_map/prf,qdf->pqrd/dot_general | solution.py:110
  97.8 0.0 all-reduce.5.cloned.1.call-update
  97.9 0.0 all-reduce.7.cloned.1.call-start
  97.9 224.1 %all-reduce.5.cloned.1.call-done = (bf16[2,256,3072]{2,1,0:T(8,128)(2,1)}, bf16[2,256,3072]{2,1,0:T(8,128)(2,1)}) async-done(((bf16[2,256,3072]{2,1,0:T(8,128)(2,1)}, bf16[2,256,3072]{2,1,0:T(8,128)(2,1)}), (bf16[2,256,3072]{2,1,0:T(8,128)(2,1)}, bf16[2,256,3072]{2,1,0:T(8,128)(2,1)})) %all-reduce.5.cloned.1.call-update) | async-done | bytes 6291472 | tf_op jit(solution)/shard_map/psum | solution.py:10
  322.0 0.0 all-reduce.7.cloned.1.call-update
  322.1 33.8 %all-reduce.7.cloned.1.call-done = (bf16[2,256,3072]{2,1,0:T(8,128)(2,1)}, bf16[2,256,3072]{2,1,0:T(8,128)(2,1)}) async-done(((bf16[2,256,3072]{2,1,0:T(8,128)(2,1)}, bf16[2,256,3072]{2,1,0:T(8,128)(2,1)}), (bf16[2,256,3072]{2,1,0:T(8,128)(2,1)}, bf16[2,256,3072]{2,1,0:T(8,128)(2,1)})) %all-reduce.7.cloned.1.call-update) | async-done | bytes 6291472 | tf_op jit(solution)/shard_map/psum | solution.py:11
  355.8 2.7 convert_convert_fusion
  358.5 3.8 all-to-all-start.3
  362.3 0.0 copy-start.2
  362.3 8.5 %convert_bitcast_fusion = bf16[1,1024,3072]{2,1,0:T(8,128)(2,1)} fusion(bf16[512,1024]{1,0:T(8,128)(2,1)} %copy-done.10, bf16[512,3072]{1,0:T(8,128)(2,1)} %bitcast.121), kind=kOutput, calls=%fused_computation.12 | convolution fusion | flops 3224371200 | bytes 10485760 | tf_op jit(solution)/shard_map/rf,rd->fd/dot_general | solution.py:99
  370.9 1.3 convert_convert_fusion.1
  372.2 9.2 %all-to-all-done.3 = bf16[4,64,3072]{2,1,0:T(8,128)(2,1)S(1)} async-done(((bf16[4,64,3072]{2,1,0:T(8,128)(2,1)}), bf16[4,64,3072]{2,1,0:T(8,128)(2,1)S(1)}, u32[]{:S(2)}, u32[]{:S(2)}) %all-to-all-start.3) | async-done | bytes 1572896 | tf_op jit(solution)/shard_map/all_to_all | solution.py:61
  381.3 4.4 all-to-all-start.1
  385.7 0.0 copy-start.8
  385.7 8.5 %convert_bitcast_fusion.1 = bf16[1,3072,1024]{2,1,0:T(8,128)(2,1)} fusion(bf16[512,3072]{1,0:T(8,128)(2,1)} %bitcast.117, bf16[512,1024]{1,0:T(8,128)(2,1)} %copy-done.9), kind=kOutput, calls=%fused_computation.13 | convolution fusion | flops 3224371200 | bytes 10485760 | tf_op jit(solution)/shard_map/rd,rf->df/dot_general | solution.py:105
  394.3 5.4 %convert_bitcast_fusion.2 = bf16[1,3072,1024]{2,1,0:T(8,128)(2,1)} fusion(bf16[512,3072]{1,0:T(8,128)(2,1)S(1)} %bitcast.119, bf16[512,1024]{1,0:T(8,128)(2,1)S(1)} %copy-done.8), kind=kOutput, calls=%fused_computation.14 | convolution fusion | flops 3224371200 | bytes 10485760 | tf_op jit(solution)/shard_map/rd,rf->df/dot_general | solution.py:102
  399.6 1.6 fusion.28
  401.2 3.3 all-to-all-done.1
  404.5 2.0 multiply_reduce_fusion
  406.5 0.3 fusion.20
  406.8 1.6 fusion.19
  408.5 28.0 %psum.39 = bf16[3072,4]{0,1:T(4,128)(2,1)S(1)} all-reduce(bf16[3072,4]{0,1:T(4,128)(2,1)S(1)} %fusion.20), channel_id=1, replica_groups=mesh['dp'=2,'expert'=4,'mp'=4] {'dp','expert'}, use_global_device_ids=true, to_apply=%region_10.11 | all-reduce | flops 12288 | bytes 49152 | tf_op jit(solution)/shard_map/psum | solution.py:91
  436.5 0.6 convert_element_type.116
  437.1 0.9 fusion.24
  (31 shorter events, 0.1 us)
Async XLA Ops:
  7.2 1.0 copy-start
  7.2 50.8 %all-gather.5.cloned.1.call-start = ((), (), s32[]{:S(2)}) async-start(), calls=%async_computation.5 | async-start | bytes 4718592 | tf_op jit(solution)/shard_map/all_gather | solution.py:50
  36.9 36.4 %all-gather.3.cloned.1.call-start = ((), (), s32[]{:S(2)}) async-start(), calls=%async_computation.4 | async-start | bytes 4718592 | tf_op jit(solution)/shard_map/all_gather | solution.py:50
  57.9 264.1 %all-reduce.5.cloned.1.call-start = ((), (), s32[]{:S(2)}) async-start(), calls=%async_computation.6 | async-start | bytes 12582912 | tf_op jit(solution)/shard_map/psum | solution.py:10
  58.0 22.0 %slice-start.4 = ((s8[6291456]{0:T(1024)(128)(4,1)}), s8[2097152]{0:T(1024)(128)(4,1)S(1)}, s32[]{:S(2)}) async-start(s8[6291456]{0:T(1024)(128)(4,1)} %bitcast.114), calls=%async_computation.12 | async-start | bytes 4194304
  73.3 6.8 %slice-start.5 = ((s8[6291456]{0:T(1024)(128)(4,1)}), s8[4194304]{0:T(1024)(128)(4,1)S(1)}, s32[]{:S(2)}) async-start(s8[6291456]{0:T(1024)(128)(4,1)} %bitcast.114), calls=%async_computation.13 | async-start | bytes 8388608
  73.3 6.8 %copy-start.5 = (bf16[8,64,3072]{2,1,0:T(8,128)(2,1)S(1)}, bf16[8,64,3072]{2,1,0:T(8,128)(2,1)}, u32[]{:S(2)}) copy-start(bf16[8,64,3072]{2,1,0:T(8,128)(2,1)} %all-gather.3.cloned.1.call-done) | copy-start | bytes 9437188
  73.3 6.8 %copy-start.11 = (f32[512,1024]{1,0:T(8,128)S(1)}, f32[512,1024]{1,0:T(8,128)}, u32[]{:S(2)}) copy-start(f32[512,1024]{1,0:T(8,128)} %fusion.6) | copy-start | bytes 6291460
  73.3 11.3 %slice-start = ((s8[6291456]{0:T(1024)(128)(4,1)}), s8[4194304]{0:T(1024)(128)(4,1)S(1)}, s32[]{:S(2)}) async-start(s8[6291456]{0:T(1024)(128)(4,1)} %bitcast.110), calls=%async_computation.8 | async-start | bytes 8388608
  73.3 14.8 %slice-start.2 = ((s8[6291456]{0:T(1024)(128)(4,1)}), s8[4194304]{0:T(1024)(128)(4,1)S(1)}, s32[]{:S(2)}) async-start(s8[6291456]{0:T(1024)(128)(4,1)} %bitcast.112), calls=%async_computation.10 | async-start | bytes 8388608
  80.1 4.4 slice-start.1
  80.1 7.9 %slice-start.3 = ((s8[6291456]{0:T(1024)(128)(4,1)}), s8[2097152]{0:T(1024)(128)(4,1)S(1)}, s32[]{:S(2)}) async-start(s8[6291456]{0:T(1024)(128)(4,1)} %bitcast.112), calls=%async_computation.11 | async-start | bytes 4194304
  84.5 3.5 copy-start.9
  84.5 3.5 copy-start.10
  84.5 8.3 %copy-start.7 = (bf16[512,1024]{1,0:T(8,128)(2,1)}, bf16[512,1024]{1,0:T(8,128)(2,1)S(1)}, u32[]{:S(2)}) copy-start(bf16[512,1024]{1,0:T(8,128)(2,1)S(1)} %get-tuple-element.12) | copy-start | bytes 3145732
  97.9 258.0 %all-reduce.7.cloned.1.call-start = ((), (), s32[]{:S(2)}) async-start(), calls=%async_computation.7 | async-start | bytes 12582912 | tf_op jit(solution)/shard_map/psum | solution.py:11
  355.8 6.5 %copy-start.4 = (s32[64,2]{0,1:T(2,128)S(1)}, s32[64,2]{0,1:T(2,128)}, u32[]{:S(2)}) copy-start(s32[64,2]{0,1:T(2,128)} %param.10) | copy-start | bytes 1540
  358.5 22.8 %all-to-all-start.3 = ((bf16[4,64,3072]{2,1,0:T(8,128)(2,1)}), bf16[4,64,3072]{2,1,0:T(8,128)(2,1)S(1)}, u32[]{:S(2)}, u32[]{:S(2)}) async-start(bf16[4,64,3072]{2,1,0:T(8,128)(2,1)} %bitcast.107), calls=%async_computation.3 | async-start | bytes 3145728 | tf_op jit(solution)/shard_map/all_to_all | solution.py:61
  362.3 8.6 %copy-start.2 = (bf16[2,256,3072]{2,1,0:T(8,128)(2,1)S(1)}, bf16[2,256,3072]{2,1,0:T(8,128)(2,1)}, u32[]{:S(2)}) copy-start(bf16[2,256,3072]{2,1,0:T(8,128)(2,1)} %get-tuple-element.8) | copy-start | bytes 9437188
  381.3 23.1 %all-to-all-start.1 = ((bf16[4,64,3072]{2,1,0:T(8,128)(2,1)}), bf16[4,64,3072]{2,1,0:T(8,128)(2,1)}, u32[]{:S(2)}, u32[]{:S(2)}) async-start(bf16[4,64,3072]{2,1,0:T(8,128)(2,1)} %bitcast.106), calls=%async_computation.1 | async-start | bytes 3145728 | tf_op jit(solution)/shard_map/all_to_all | solution.py:61
  385.7 8.5 %copy-start.6 = (bf16[8,64,3072]{2,1,0:T(8,128)(2,1)S(1)}, bf16[8,64,3072]{2,1,0:T(8,128)(2,1)}, u32[]{:S(2)}) copy-start(bf16[8,64,3072]{2,1,0:T(8,128)(2,1)} %all-gather.3.cloned.1.call-done) | copy-start | bytes 9437188
  385.7 8.5 %copy-start.8 = (bf16[512,1024]{1,0:T(8,128)(2,1)S(1)}, bf16[512,1024]{1,0:T(8,128)(2,1)}, u32[]{:S(2)}) copy-start(bf16[512,1024]{1,0:T(8,128)(2,1)} %copy-done.7) | copy-start | bytes 3145732
  399.6 7.2 %copy-start.3 = (f32[3072,4]{0,1:T(4,128)S(1)}, f32[3072,4]{0,1:T(4,128)}, u32[]{:S(2)}) copy-start(f32[3072,4]{0,1:T(4,128)} %param.9) | copy-start | bytes 147460
  404.5 2.3 copy-start.1
Sparse Core Ops, SparseCore 0:
  37.0 13.7 all-gather.4
  58.1 15.1 all-gather.2
  98.0 224.0 all-reduce.4
  324.4 31.3 all-reduce.6
